TPU v7x, 512 devices: a whole 4x8x8 slice. The times are simulated.
512 devices in a mesh: tile: 32 (over z, x), node: 16 (over y, core).
Axes of the slice: x: 4, y: 8, z: 8, core: 2. Of those that a mesh axis runs over, the one named last changes fastest.
Arguments:
- features: bfloat16 [262144, 768], P(('tile', 'node')), may hold values from -6 to 6
- target_features: bfloat16 [131072, 768], P(('tile', 'node')), may hold values from -6 to 6
- counts: int32 [512, 2, 6, 256, 256], P(('tile', 'node')), may hold values from 0 to 7
- send_slot: int32 [512, 32, 1], P(('tile', 'node')), may hold values from 0 to 1
- tile_from: int32 [512, 2, 6], P(('tile', 'node')), may hold values from 0 to 31, as said below
- projection: bfloat16 [2304, 768], P('node'), may hold values from -0.125 to 0.125
Outputs:
- projected: bfloat16 [131072, 768], P(('tile', 'node'))
Inputs may be any that keep to these rules, and one draw needn't show every extreme that they name: `send_slot`: A local block index of the sending device. `tile_from`: slot q * 1 + c is slot c sent by the device at tile index q in the same node group. The 12 entries of one device name distinct slots where there are that many slots; otherwise every slot is named.
All inputs are finite; a program needn't handle non-finite values.
Results may differ from a plain program's by a relative error of at most 0.0034.
Values may be sent and summed in bfloat16 or wider, within the bound.
No kernel may reach another device: no remote copies, remote signals or barrier semaphores. Data moves between devices by JAX's collectives and lax.ppermute only.
A program may use at most 128 MiB of HBM per device.

v0:
```python
import math

import jax
import jax.numpy as jnp
from jax import lax
from jax.sharding import PartitionSpec as P


def shards(features, target_features, counts, send_slot, tile_from, projection):
    block_rows = counts.shape[-1]
    width = features.shape[1]
    blocks = features.reshape(-1, block_rows, width)
    outgoing = jnp.take(blocks, send_slot.reshape(-1), axis=0)
    incoming = lax.all_to_all(outgoing, "tile", split_axis=0, concat_axis=0, tiled=True)
    picked = jnp.take(incoming, tile_from.reshape(-1), axis=0).reshape(2, -1, block_rows, width)
    tile_weights = counts[0].astype(jnp.bfloat16)
    diffused = jnp.einsum(
        "klts,klsf->ktf", tile_weights, picked, preferred_element_type=jnp.float32
    )
    scaling = 1.0 / (8.0 * math.sqrt(block_rows * counts.shape[2]))
    diffused = (diffused * scaling).astype(jnp.bfloat16)
    stacked = jnp.concatenate([target_features, diffused[0], diffused[1]], axis=1)
    result = jnp.dot(
        stacked,
        lax.all_gather(projection, "node", axis=0, tiled=True),
        preferred_element_type=jnp.float32,
    )
    return result.astype(jnp.bfloat16)


def solution(mesh):
    placed = (
        P(("tile", "node"), None),
        P(("tile", "node"), None),
        P(("tile", "node"), None, None, None, None),
        P(("tile", "node"), None, None),
        P(("tile", "node"), None, None),
        P("node", None),
    )
    return jax.shard_map(
        shards, mesh=mesh, in_specs=placed, out_specs=P(("tile", "node"), None), check_vma=False
    )
```

profile of v0, /device:TPU:6, one launch (start us, length us, event | category | flops | bytes accessed | tf_op | source)
XLA Modules:
  0.0 371.1 jit_solution(5701685780761236654)
XLA Ops:
  6.5 0.0 copy-start
  6.5 0.7 fusion.21
  7.3 0.7 compare_and_fusion
  7.9 0.0 copy-done
  7.9 6.4 %gather_fusion = bf16[32,256,768]{2,1,0:T(8,128)(2,1)} fusion(bf16[2,256,768]{2,1,0:T(8,128)(2,1)S(1)} %bitcast.33, s32[1024]{0:T(1024)S(1)} %pad_clamp_fusion.1), kind=kCustom, calls=%fused_computation | custom fusion | bytes 25165952 | tf_op jit(solution)/shard_map/jit(_take)/gather | solution.py:13
  14.4 10.9 %broadcast_select_fusion = bf16[32,256,768]{2,1,0:T(8,128)(2,1)} fusion(bf16[32,256,768]{2,1,0:T(8,128)(2,1)} %gather_fusion, pred[32]{0:T(512)(128)(4,1)S(1)} %compare_and_fusion), kind=kLoop, calls=%fused_computation.2 | loop fusion | flops 6291456 | bytes 25165856 | tf_op jit(solution)/shard_map/jit(_take)/select_n | solution.py:13
  25.2 0.0 copy-start.2
  25.2 0.0 copy-start.1
  25.2 13.7 %all-to-all-start = ((bf16[32,256,768]{2,1,0:T(8,128)(2,1)}), bf16[32,256,768]{2,1,0:T(8,128)(2,1)}, u32[]{:S(2)}, u32[]{:S(2)}) async-start(bf16[32,256,768]{2,1,0:T(8,128)(2,1)} %broadcast_select_fusion), calls=%async_computation | async-start | bytes 25165824 | tf_op jit(solution)/shard_map/all_to_all | solution.py:14
  39.0 0.0 all-gather.2.cloned.1.call-start
  39.0 0.7 all-gather.2.cloned.1.call-update
  39.7 0.0 copy-done.2
  39.7 0.1 reshape.90
  39.8 0.0 copy-done.1
  39.8 0.2 copy.8
  40.0 301.2 %all-to-all-done = bf16[32,256,768]{2,1,0:T(8,128)(2,1)} async-done(((bf16[32,256,768]{2,1,0:T(8,128)(2,1)}), bf16[32,256,768]{2,1,0:T(8,128)(2,1)}, u32[]{:S(2)}, u32[]{:S(2)}) %all-to-all-start) | async-done | bytes 12582944 | tf_op jit(solution)/shard_map/all_to_all | solution.py:14
  341.2 7.7 %gather_fusion.1 = bf16[12,256,768]{2,1,0:T(8,128)(2,1)} fusion(bf16[32,256,768]{2,1,0:T(8,128)(2,1)} %all-to-all-done, s32[1024]{0:T(1024)S(1)} %pad_clamp_fusion), kind=kCustom, calls=%fused_computation.1 | custom fusion | bytes 9437232 | tf_op jit(solution)/shard_map/jit(_take)/gather | solution.py:15
  348.9 6.6 %copy.7 = bf16[12,256,768]{1,2,0:T(8,128)(2,1)} copy(bf16[12,256,768]{2,1,0:T(8,128)(2,1)} %gather_fusion.1) | data formatting | bytes 9437184 | tf_op jit(solution)/shard_map/jit(_take)/gather | solution.py:15
  355.5 4.8 %fusion.11 = bf16[2,256,768]{1,2,0:T(8,128)(2,1)S(1)} fusion(s32[1,2,6,256,256]{4,3,2,1,0:T(8,128)} %param.8, bf16[2,6,256,768]{2,3,1,0:T(8,128)(2,1)} %bitcast.34, pred[2,6]{1,0:T(4,128)(4,1)S(1)} %compare_and_fusion.1), kind=kOutput, calls=%fused_computation.11 | convolution fusion | flops 1211891712 | bytes 8650764 | tf_op jit(solution)/shard_map/klts,klsf->ktf/dot_general | solution.py:17
  360.3 0.1 slice_bitcast_fusion.1
  360.3 0.0 all-gather.2.cloned.1.call-done
  360.4 3.9 %convolution_convert_fusion = bf16[256,768]{1,0:T(8,128)(2,1)} fusion(bf16[2304,768]{1,0:T(8,128)(2,1)} %all-gather.2.cloned.1.call-done, bf16[256,768]{0,1:T(8,128)(2,1)S(1)} %get-tuple-element.6, bf16[256,768]{0,1:T(8,128)(2,1)S(1)} %get-tuple-element.5, bf16[256,768]{0,1:T(8,128)(2,1)S(1)} %copy.8), kind=kOutput, calls=%fused_computation.12 | convolution fusion | flops 909705216 | bytes 5111808 | tf_op jit(solution)/shard_map/dot_general | solution.py:23
  (4 shorter events, 0.0 us)
Async XLA Ops:
  6.5 1.4 copy-start
  25.2 14.4 %copy-start.2 = (s32[1,2,6]{2,1,0:T(2,128)S(1)}, s32[1,2,6]{2,1,0:T(2,128)}, u32[]{:S(2)}) copy-start(s32[1,2,6]{2,1,0:T(2,128)} %param.10) | copy-start | bytes 148
  25.2 14.5 %copy-start.1 = (bf16[256,768]{1,0:T(8,128)(2,1)S(1)}, bf16[256,768]{1,0:T(8,128)(2,1)}, u32[]{:S(2)}) copy-start(bf16[256,768]{1,0:T(8,128)(2,1)} %param.7) | copy-start | bytes 1179652
  25.2 316.0 %all-to-all-start = ((bf16[32,256,768]{2,1,0:T(8,128)(2,1)}), bf16[32,256,768]{2,1,0:T(8,128)(2,1)}, u32[]{:S(2)}, u32[]{:S(2)}) async-start(bf16[32,256,768]{2,1,0:T(8,128)(2,1)} %broadcast_select_fusion), calls=%async_computation | async-start | bytes 25165824 | tf_op jit(solution)/shard_map/all_to_all | solution.py:14
  39.0 321.4 %all-gather.2.cloned.1.call-start = ((), (), s32[]{:S(2)}) async-start(), calls=%async_computation.1 | async-start | bytes 3760128 | tf_op jit(solution)/shard_map/all_gather | solution.py:25
Sparse Core Ops, SparseCore 0:
  41.9 44.6 all-gather.1
where the time goes:
time: 372 us; the launch traced here: 371 us
  waiting for transfers between devices  302 us (81%)
  local copies, waits for them, and re-layouts  21.1 us (6%)
  starting transfers between devices  13.7 us (4%)
  between operations  13.5 us (4%)
  other arithmetic  12.3 us (3%)
  matrix products  8.63 us (2%)
    all_to_all x1, waiting for transfers between devices, shards(): lax.all_to_all(outgoing, 'tile', split_axis=0, concat_axis=0, tiled=True)  301 us
    gather x2, local copies, waits for them, and re-layouts, shards(): jnp.take(incoming, tile_from.reshape(-1), axis=0)  14.3 us
    all_to_all x1, starting transfers between devices, shards(): lax.all_to_all(outgoing, 'tile', split_axis=0, concat_axis=0, tiled=True)  13.7 us
    select_n x2, other arithmetic, shards(): outgoing = jnp.take(blocks, send_slot.reshape(-1), axis=0)  11.6 us
  transfers between devices with their start and end apart: 2, of which 1 were waited for; matrix products, arithmetic and copies ran while one was open for 5% of the time, Pallas kernels for 0%

commit v1 on v0

v1 whole, which is shorter than its diff:
```python
import functools
import math

import jax
import jax.numpy as jnp
from jax import lax
from jax.experimental import pallas as pl
from jax.experimental.pallas import tpu as pltpu
from jax.sharding import PartitionSpec as P

NX = 4
NZ = 8
META = 8
LIFT = 2.0**13


def z_groups():
    return [[z * NX + x for z in range(NZ)] for x in range(NX)]


def x_groups():
    return [[z * NX + x for x in range(NX)] for z in range(NZ)]


def sort_kernel(slot_ref, counts_ref, out_ref):
    t = pl.program_id(0)
    rows = counts_ref.shape[-1]
    operator_tiles = pl.num_programs(0) // 2

    @pl.when(t == 0)
    def _():
        out_ref[:, pl.ds(NZ * rows, META), :] = jnp.zeros((NX, META, rows), jnp.bfloat16)

    slot = slot_ref[t]
    z, x = slot // NX, slot % NX
    tile = counts_ref[...].reshape(rows, rows)
    out_ref[x, pl.ds(pl.multiple_of(z * rows, rows), rows), :] = tile.astype(jnp.float32).astype(jnp.bfloat16)
    lane = lax.broadcasted_iota(jnp.int32, (META, rows), 1)
    code = jnp.where(t < operator_tiles, 1.0, 2.0)
    mark = jnp.where(lane == z, code, 0.0)
    old = out_ref[x, pl.ds(NZ * rows, META), :].astype(jnp.float32)
    out_ref[x, pl.ds(NZ * rows, META), :] = (old + mark).astype(jnp.bfloat16)


def sort_tiles(counts, slots):
    tiles, rows = slots.shape[0], counts.shape[-1]
    return pl.pallas_call(
        sort_kernel,
        out_shape=jax.ShapeDtypeStruct((NX, NZ * rows + META, rows), jnp.bfloat16),
        grid_spec=pltpu.PrefetchScalarGridSpec(
            num_scalar_prefetch=1,
            grid=(tiles,),
            in_specs=[pl.BlockSpec((1, rows, rows), lambda t, s: (t, 0, 0))],
            out_specs=pl.BlockSpec((NX, NZ * rows + META, rows), lambda t, s: (0, 0, 0)),
        ),
        name="sort_tiles",
    )(slots, counts.reshape(tiles, rows, rows))


def partial_kernel(scaling, meta_ref, w_ref, f_ref, p_ref, t_ref, sent_ref, own_ref, acc_ref):
    rows, width = t_ref.shape
    x = meta_ref[2 * NX * NZ]

    def diffuse(xd):
        acc_ref[...] = jnp.zeros_like(acc_ref)

        def source(z, carry):
            code = meta_ref[xd * NZ + z]
            block = meta_ref[NX * NZ + xd * NZ + z]

            @pl.when(code > 0)
            def _():
                w = w_ref[xd, pl.ds(pl.multiple_of(z * rows, rows), rows), :]
                f = f_ref[z, pl.ds(pl.multiple_of(block * rows, rows), rows), :]
                acc_ref[code - 1] += jnp.dot(w, f, preferred_element_type=jnp.float32)

            return carry

        lax.fori_loop(0, NZ, source, 0)
        total = None
        for k in range(2):
            d = (acc_ref[k] * scaling).astype(jnp.bfloat16)
            part = jnp.dot(d, p_ref[pl.ds((k + 1) * width, width), :], preferred_element_type=jnp.float32)
            total = part if total is None else total + part
        return total

    def remote(r, carry):
        xd = lax.rem(x + r, NX)
        sent_ref[xd] = diffuse(xd).astype(jnp.bfloat16)
        return carry

    lax.fori_loop(1, NX, remote, 0)
    sent_ref[x] = jnp.zeros((rows, sent_ref.shape[-1]), jnp.bfloat16)
    own_ref[...] = diffuse(x) + jnp.dot(
        t_ref[...], p_ref[pl.ds(0, width), :], preferred_element_type=jnp.float32
    )


def shards(features, target_features, counts, send_slot, tile_from, projection):
    rows, width = counts.shape[-1], features.shape[1]
    out_width = projection.shape[1]
    scaling = 1.0 / (8.0 * math.sqrt(rows * counts.shape[2]))
    me = lax.axis_index("tile")
    my_z, my_x = me // NX, me % NX

    whole_projection = lax.all_gather(projection, "node", axis=0, tiled=True)

    sorted_tiles = sort_tiles(counts, tile_from.reshape(-1))
    tiles = lax.all_to_all(sorted_tiles, "tile", 0, 0, axis_index_groups=x_groups(), tiled=True)

    extra = jnp.pad(send_slot.reshape(1, -1).astype(jnp.float32), ((0, META - 1), (0, width - send_slot.shape[1])))
    payload = jnp.concatenate([features.astype(jnp.float32) * LIFT, extra], axis=0).astype(jnp.float16)
    column = lax.all_gather(payload, "tile", axis=0, tiled=False, axis_index_groups=z_groups())
    blocks = (column[:, :-META].astype(jnp.float32) * (1.0 / LIFT)).astype(jnp.bfloat16)

    picks = lax.dynamic_slice(column[:, -META, :], (0, my_z * NX), (NZ, NX))
    codes = tiles[:, NZ * rows, :NZ]
    meta = jnp.concatenate([
        codes.astype(jnp.int32).reshape(-1),
        picks.astype(jnp.int32).T.reshape(-1),
        my_x.astype(jnp.int32).reshape(1),
    ])
    vmem = pl.BlockSpec(memory_space=pltpu.VMEM)
    sent, own = pl.pallas_call(
        functools.partial(partial_kernel, scaling),
        out_shape=(
            jax.ShapeDtypeStruct((NX, rows, out_width), jnp.bfloat16),
            jax.ShapeDtypeStruct((rows, out_width), jnp.float32),
        ),
        in_specs=[pl.BlockSpec(memory_space=pltpu.SMEM), vmem, vmem, vmem, vmem],
        out_specs=(vmem, vmem),
        scratch_shapes=[pltpu.VMEM((2, rows, width), jnp.float32)],
        name="partial_sums",
    )(meta, tiles, blocks, whole_projection, target_features)
    received = lax.all_to_all(sent, "tile", 0, 0, axis_index_groups=x_groups(), tiled=True)
    return (own + received.astype(jnp.float32).sum(0)).astype(jnp.bfloat16)


def solution(mesh):
    placed = (
        P(("tile", "node"), None),
        P(("tile", "node"), None),
        P(("tile", "node"), None, None, None, None),
        P(("tile", "node"), None, None),
        P(("tile", "node"), None, None),
        P("node", None),
    )
    return jax.shard_map(
        shards, mesh=mesh, in_specs=placed, out_specs=P(("tile", "node"), None), check_vma=False
    )
```

time: 372 us -> 152 us (0.41)
  the two profiles are of different devices: /device:TPU:6 before, /device:TPU:24 now
where the time goes in v1:
time: 152 us
  blocking collectives  95.7 us (63%)
  Pallas kernels  23.1 us (15%)
  between operations  13.5 us (9%)
  other arithmetic  9.47 us (6%)
  starting transfers between devices  5.06 us (3%)
  local copies, waits for them, and re-layouts  4.36 us (3%)
    all_gather x1, blocking collectives, shards(): lax.all_gather(payload, 'tile', axis=0, tiled=False, axis_index_groups=z_...  70.5 us
    all_to_all x1, blocking collectives, shards(): lax.all_to_all(sent, 'tile', 0, 0, axis_index_groups=x_groups(), tiled=True)  25.2 us
    pallas_call x1, Pallas kernels, shards(): pl.pallas_call(functools.partial(partial_kernel, scaling), out_shape=(jax...  14.5 us
    pallas_call x1, Pallas kernels, sort_tiles(): pl.pallas_call(sort_kernel, out_shape=jax.ShapeDtypeStruct((NX, NZ * rows...  8.68 us
    convert_element_type x1, other arithmetic, shards(): (column[:, :-META].astype(jnp.float32) * (1.0 / LIFT)).astype(jnp.bfloat16)  6.73 us
    all_to_all x1, starting transfers between devices, shards(): lax.all_to_all(sorted_tiles, 'tile', 0, 0, axis_index_groups=x_groups(),...  5.05 us
  transfers between devices with their start and end apart: 2, of which 0 were waited for; matrix products, arithmetic and copies ran while one was open for 7% of the time, Pallas kernels for 6%

profile of v1, /device:TPU:24, one launch (start us, length us, event | category | flops | bytes accessed | tf_op | source)
XLA Modules:
  0.0 152.0 jit_solution(18353035232046305982)
XLA Ops:
  6.5 0.0 all-gather.3.cloned.1.call-start
  6.5 0.7 all-gather.3.cloned.1.call-update
  7.3 1.3 reshape.68.slot_ref
  8.5 8.7 %sort_tiles.1 = bf16[4,2056,256]{2,1,0:T(8,128)(2,1)} custom-call(s32[12]{0:T(128)} %reshape.68.slot_ref, s32[12,256,256]{2,1,0:T(8,128)} %bitcast.13), custom_call_target="tpu_custom_call" | custom-call | tf_op jit(solution)/shard_map/sort_tiles/pallas_call | solution.py:47
  17.2 0.0 copy-start.3
  17.2 0.0 copy-start.1
  17.2 5.1 %all-to-all-start = ((bf16[4,2056,256]{2,1,0:T(8,128)(2,1)}), bf16[4,2056,256]{2,1,0:T(8,128)(2,1)}, u32[]{:S(2)}, u32[]{:S(2)}) async-start(bf16[4,2056,256]{2,1,0:T(8,128)(2,1)} %sort_tiles.1), calls=%async_computation | async-start | bytes 8421376 | tf_op jit(solution)/shard_map/all_to_all | solution.py:109
  22.3 0.0 copy-done.3
  22.3 0.0 copy-done.1
  22.3 0.2 fusion
  22.5 0.2 pad_maximum_fusion
  22.7 70.5 %all-gather.4 = f16[8,520,768]{2,1,0:T(8,128)(2,1)S(1)} all-gather(f16[1,520,768]{2,1,0:T(8,128)(2,1)S(1)} %pad_maximum_fusion), channel_id=1, replica_groups={{0,64,128,192,256,320,384,448},{16,80,144,208,272,336,400,464},{32,96,1..., dimensions={0}, use_global_device_ids=true | all-gather | bytes 7188480 | tf_op jit(solution)/shard_map/all_gather | solution.py:113
  93.3 0.0 copy-start
  93.3 2.7 %copy-done = f16[8,520,768]{2,1,0:T(8,128)(2,1)} copy-done((f16[8,520,768]{2,1,0:T(8,128)(2,1)}, f16[8,520,768]{2,1,0:T(8,128)(2,1)S(1)}, u32[]{:S(2)}) %copy-start) | copy-done | bytes 6389784
  96.0 0.1 constant_dynamic-slice_fusion
  96.1 0.1 copy.10
  96.2 0.1 reshape.75
  96.3 6.7 %multiply_convert_fusion.f_ref = bf16[8,512,768]{2,1,0:T(8,128)(2,1)} fusion(f16[8,520,768]{2,1,0:T(8,128)(2,1)} %copy-done), kind=kLoop, calls=%fused_computation | loop fusion | flops 9437184 | bytes 12582912 | tf_op jit(solution)/shard_map/convert_element_type | solution.py:114
  103.0 0.0 all-to-all-done.w_ref
  103.0 0.7 fusion.1
  103.7 0.1 reshape.73
  103.8 0.6 pad_add_fusion.meta_ref
  104.4 0.0 all-gather.3.cloned.1.call-done.p_ref
  104.4 14.5 %partial_sums.1 = (bf16[4,256,768]{2,1,0:T(8,128)(2,1)}, f32[256,768]{1,0:T(8,128)}) custom-call(s32[65]{0:T(128)} %pad_add_fusion.meta_ref, bf16[4,2056,256]{2,1,0:T(8,128)(2,1)} %all-to-all-done.w_ref, bf16[8,512,768]{2,1,0:T(8,128)(2,1)} %multiply_convert_fusion.f_ref, bf16[2304,768]{1,0:T(8,128)(2,1)} %all-gather.3.cloned.1.call-done.p_ref, ...), custom_call_target="tpu_custom_call" | custom-call | tf_op jit(solution)/shard_map/partial_sums/pallas_call | solution.py:124
  118.9 0.0 copy-start.2
  118.9 25.2 %all_to_all.10 = bf16[4,256,768]{2,1,0:T(8,128)(2,1)S(1)} all-to-all(bf16[4,256,768]{2,1,0:T(8,128)(2,1)} %get-tuple-element.8), channel_id=1, replica_groups={{0,16,32,48},{64,80,96,112},{128,144,160,176},{192,208,224,240},{256,27..., dimensions={0} | all-to-all | bytes 3145728 | tf_op jit(solution)/shard_map/all_to_all | solution.py:135
  144.1 0.2 convert_reduce_fusion
  144.3 0.0 copy-done.2
  144.3 0.8 add_convert_fusion
  (4 shorter events, 0.0 us)
Async XLA Ops:
  6.5 97.9 %all-gather.3.cloned.1.call-start = ((), (), s32[]{:S(2)}) async-start(), calls=%async_computation.2 | async-start | bytes 3760128 | tf_op jit(solution)/shard_map/all_gather | solution.py:106
  17.2 5.1 %copy-start.3 = (s32[1,32,1]{1,2,0:T(1,128)S(1)}, s32[1,32,1]{1,2,0:T(1,128)}, u32[]{:S(2)}) copy-start(s32[1,32,1]{1,2,0:T(1,128)} %param.9) | copy-start | bytes 388
  17.2 5.1 %copy-start.1 = (bf16[512,768]{1,0:T(8,128)(2,1)S(1)}, bf16[512,768]{1,0:T(8,128)(2,1)}, u32[]{:S(2)}) copy-start(bf16[512,768]{1,0:T(8,128)(2,1)} %param.6) | copy-start | bytes 2359300
  17.2 85.8 %all-to-all-start = ((bf16[4,2056,256]{2,1,0:T(8,128)(2,1)}), bf16[4,2056,256]{2,1,0:T(8,128)(2,1)}, u32[]{:S(2)}, u32[]{:S(2)}) async-start(bf16[4,2056,256]{2,1,0:T(8,128)(2,1)} %sort_tiles.1), calls=%async_computation | async-start | bytes 8421376 | tf_op jit(solution)/shard_map/all_to_all | solution.py:109
  93.3 2.7 %copy-start = (f16[8,520,768]{2,1,0:T(8,128)(2,1)}, f16[8,520,768]{2,1,0:T(8,128)(2,1)S(1)}, u32[]{:S(2)}) copy-start(f16[8,520,768]{2,1,0:T(8,128)(2,1)S(1)} %all-gather.4) | copy-start | bytes 19169284
  118.9 25.4 %copy-start.2 = (f32[256,768]{1,0:T(8,128)S(1)}, f32[256,768]{1,0:T(8,128)}, u32[]{:S(2)}) copy-start(f32[256,768]{1,0:T(8,128)} %get-tuple-element.7) | copy-start | bytes 2359300
Sparse Core Ops, SparseCore 0:
  9.5 47.7 all-gather.2
